TPU v7x, 32 devices: a whole 2x2x4 slice. The times are simulated.
32 devices in a mesh: groups: 2 (over y), rows: 4 (over z), feat: 4 (over x, core).
Axes of the slice: x: 2, y: 2, z: 4, core: 2. Of those that a mesh axis runs over, the one named last changes fastest.
Arguments:
- student: float32 [1280, 4096], P(('groups', 'rows'), 'feat'), parts along dimension 0, may hold values from -1 to 1
- teacher: bfloat16 [1280, 1024], P(('groups', 'rows'), 'feat'), parts along dimension 0, may hold values from -1 to 1
Outputs:
- row_loss: float32 [1280], P(('groups', 'rows')), parts along dimension 0
- student_grad: float32 [1280, 4096], P(('groups', 'rows'), 'feat'), parts along dimension 0
There are 2 independent parts, one for each index of `groups`. A program takes and returns all parts, laid end to end along the dimension named above; each array names one. Nothing has to cross between parts.
All inputs are finite; a program needn't handle non-finite values.
Results may differ from a plain program's by a relative error of at most 0.0085.
Values may be sent and summed in bfloat16 or wider, within the bound.
A program may use at most 64 MiB of HBM per device.

v0:
```python
import jax
import jax.numpy as jnp
from jax import lax
from jax.sharding import PartitionSpec as P

D = 4096


EPSILON = 1e-06


def shifted(block, axis, distance):
    devices = range(lax.axis_size(axis))
    route = [((i - distance) % len(devices), i) for i in devices]
    return lax.ppermute(block, axis, route)


def on_device(student, teacher):
    cycle = lax.axis_size("rows")
    rows_here = student.shape[0]
    width = student.shape[1]
    embeds = rows_here * cycle
    squares = lax.psum(jnp.sum(student * student, axis=1), "feat")
    scaling = lax.rsqrt(squares + EPSILON)
    unit = student * scaling[:, None]
    unit_half = unit.astype(jnp.bfloat16)
    packed = jnp.concatenate([unit_half, teacher], axis=1)
    contract = (((1,), (1,)), ((), ()))

    def absorb(carry, visitor):
        losses, pulled = carry
        other_unit = visitor[:, :width]
        other_teacher = visitor[:, width:]
        student_term = lax.dot_general(
            unit_half, other_unit, contract, preferred_element_type=jnp.float32
        )
        teacher_term = lax.dot_general(
            teacher, other_teacher, contract, preferred_element_type=jnp.float32
        )
        differ = lax.psum((student_term - teacher_term).astype(jnp.bfloat16), "feat").astype(
            jnp.float32
        )
        losses = losses + jnp.sum(differ * differ, axis=1)
        pulled = pulled + jnp.dot(
            differ.astype(jnp.bfloat16), other_unit, preferred_element_type=jnp.float32
        )
        return (losses, pulled)

    carry = (jnp.zeros((rows_here,), jnp.float32), jnp.zeros((rows_here, width), jnp.float32))
    carry = absorb(carry, packed)

    def turn(step, state):
        inner, visitor = state
        visitor = shifted(visitor, "rows", 1)
        return (absorb(inner, visitor), visitor)

    carry, visitor = lax.fori_loop(0, cycle - 1, turn, (carry, packed))
    losses, pulled = carry
    radial = lax.psum(jnp.sum(pulled * unit, axis=1), "feat")
    factor = 4.0 * D / embeds
    student_grad = factor * scaling[:, None] * (pulled - radial[:, None] * unit)
    return (D / embeds * losses, student_grad)


def solution(mesh):
    in_specs = (P(("groups", "rows"), "feat"), P(("groups", "rows"), "feat"))
    out_specs = (P(("groups", "rows")), P(("groups", "rows"), "feat"))
    return jax.shard_map(
        on_device, mesh=mesh, in_specs=in_specs, out_specs=out_specs, check_vma=False
    )
```

profile of v0, /device:TPU:0, one launch (start us, length us, event | category | flops | bytes accessed | tf_op | source)
XLA Modules:
  0.0 104.7 jit_solution(14661461870272374266)
XLA Ops:
  0.6 0.0 copy-start
  0.6 1.3 %multiply_reduce_fusion.2 = f32[160]{0:T(256)S(1)} fusion(f32[160,1024]{1,0:T(8,128)} %param.4), kind=kLoop, calls=%fused_computation.12 | loop fusion | flops 327520 | bytes 656000 | tf_op jit(solution)/shard_map/reduce_sum | solution.py:23
  1.9 8.3 %psum.28 = f32[160]{0:T(256)S(1)} all-reduce(f32[160]{0:T(256)S(1)} %multiply_reduce_fusion.2), channel_id=1, replica_groups=mesh['groups'=2,'rows'=4,'feat'=4] {'feat'}, use_global_device_ids=true, to_apply=%region_1.0 | all-reduce | flops 160 | bytes 1280 | tf_op jit(solution)/shard_map/psum | solution.py:23
  10.3 0.0 copy-done
  10.3 0.0 copy-start.1
  10.3 0.1 multiply_convert_fusion
  10.4 0.8 copy-done.1
  11.2 0.2 fusion.6
  11.3 0.3 fusion.5
  11.6 11.0 %psum.29 = bf16[160,160]{1,0:T(8,128)(2,1)S(1)} all-reduce(bf16[160,160]{1,0:T(8,128)(2,1)S(1)} %fusion.5), channel_id=1, replica_groups=mesh['groups'=2,'rows'=4,'feat'=4] {'feat'}, use_global_device_ids=true, to_apply=%region_2.0 | all-reduce | flops 25600 | bytes 102400 | tf_op jit(solution)/shard_map/psum | solution.py:40
  22.6 0.2 fusion.7
  22.8 0.1 multiply_reduce_fusion.3
  23.0 74.0 %while.14 = (s32[]{:T(128)}, f32[160]{0:T(256)S(1)}, f32[160,1024]{1,0:T(8,128)S(1)}, bf16[160,1280]{1,0:T(8,128)(2,1)S(1)}, bf16[160,1024]{1,0:T(8,128)(2,1)S(1)}, /*index=5*/bf16[160,256]{1,0:T(8,128)(2,1)S(1)}, s32[]{:T(128)}) while((s32[]{:T(128)}, f32[160]{0:T(256)S(1)}, f32[160,1024]{1,0:T(8,128)S(1)}, bf16[160,1280]{1,0:T(8,128)(2,1)S(1)}, ...), condition=%wide.region_7.0_spmd, body=%wide.region_4.0_spmd.sunk | while | flops 118282240 | bytes 5470837 | solution.py:57
  23.0 1.8 %collective-permute-start = (bf16[160,1280]{1,0:T(8,128)(2,1)S(1)}, bf16[160,1280]{1,0:T(8,128)(2,1)S(1)}, u32[]{:S(2)}, u32[]{:S(2)}) collective-permute-start(bf16[160,1280]{1,0:T(8,128)(2,1)S(1)} %get-tuple-element.98), channel_id=1, source_target_pairs={{12,0},{0,4},{4,8},{8,12},{13,1},{1,5},{5,9},{9,13},{14,2},{2,6},{... | collective-permute-start | bytes 1228808 | tf_op jit(solution)/shard_map/while/body/eval_jaxpr/ppermute | solution.py:15
  24.9 11.0 %collective-permute-done = bf16[160,1280]{1,0:T(8,128)(2,1)S(1)} collective-permute-done((bf16[160,1280]{1,0:T(8,128)(2,1)S(1)}, bf16[160,1280]{1,0:T(8,128)(2,1)S(1)}, u32[]{:S(2)}, u32[]{:S(2)}) %collective-permute-start) | collective-permute-done | bytes 409632 | tf_op jit(solution)/shard_map/while/body/eval_jaxpr/ppermute | solution.py:15
  35.9 0.2 fusion.31
  36.1 0.3 fusion.32
  36.3 11.0 %psum.32 = bf16[160,160]{1,0:T(8,128)(2,1)S(1)} all-reduce(bf16[160,160]{1,0:T(8,128)(2,1)S(1)} %fusion.32), channel_id=1, replica_groups=mesh['groups'=2,'rows'=4,'feat'=4] {'feat'}, use_global_device_ids=true, to_apply=%region_5.0 | all-reduce | flops 25600 | bytes 102400 | tf_op jit(solution)/shard_map/while/body/eval_jaxpr/psum | solution.py:40
  47.3 0.1 multiply_reduce_fusion.5
  47.5 0.2 convolution_add_fusion.2
  47.8 0.1 collective-permute-start
  47.8 12.7 %collective-permute-done = bf16[160,1280]{1,0:T(8,128)(2,1)S(1)} collective-permute-done((bf16[160,1280]{1,0:T(8,128)(2,1)S(1)}, bf16[160,1280]{1,0:T(8,128)(2,1)S(1)}, u32[]{:S(2)}, u32[]{:S(2)}) %collective-permute-start) | collective-permute-done | bytes 409632 | tf_op jit(solution)/shard_map/while/body/eval_jaxpr/ppermute | solution.py:15
  60.5 0.2 fusion.31
  60.7 0.3 fusion.32
  61.0 10.9 %psum.32 = bf16[160,160]{1,0:T(8,128)(2,1)S(1)} all-reduce(bf16[160,160]{1,0:T(8,128)(2,1)S(1)} %fusion.32), channel_id=1, replica_groups=mesh['groups'=2,'rows'=4,'feat'=4] {'feat'}, use_global_device_ids=true, to_apply=%region_5.0 | all-reduce | flops 25600 | bytes 102400 | tf_op jit(solution)/shard_map/while/body/eval_jaxpr/psum | solution.py:40
  71.9 0.1 multiply_reduce_fusion.5
  72.1 0.2 convolution_add_fusion.2
  72.3 0.1 collective-permute-start
  72.4 12.8 %collective-permute-done = bf16[160,1280]{1,0:T(8,128)(2,1)S(1)} collective-permute-done((bf16[160,1280]{1,0:T(8,128)(2,1)S(1)}, bf16[160,1280]{1,0:T(8,128)(2,1)S(1)}, u32[]{:S(2)}, u32[]{:S(2)}) %collective-permute-start) | collective-permute-done | bytes 409632 | tf_op jit(solution)/shard_map/while/body/eval_jaxpr/ppermute | solution.py:15
  85.2 0.2 fusion.31
  85.4 0.3 fusion.32
  85.7 10.9 %psum.32 = bf16[160,160]{1,0:T(8,128)(2,1)S(1)} all-reduce(bf16[160,160]{1,0:T(8,128)(2,1)S(1)} %fusion.32), channel_id=1, replica_groups=mesh['groups'=2,'rows'=4,'feat'=4] {'feat'}, use_global_device_ids=true, to_apply=%region_5.0 | all-reduce | flops 25600 | bytes 102400 | tf_op jit(solution)/shard_map/while/body/eval_jaxpr/psum | solution.py:40
  96.6 0.1 multiply_reduce_fusion.5
  96.7 0.2 convolution_add_fusion.2
  97.0 0.2 multiply_reduce_fusion.1
  97.2 5.9 %psum.30 = f32[160]{0:T(256)S(1)} all-reduce(f32[160]{0:T(256)S(1)} %multiply_reduce_fusion.1), channel_id=1, replica_groups=mesh['groups'=2,'rows'=4,'feat'=4] {'feat'}, use_global_device_ids=true, to_apply=%region_9.0 | all-reduce | flops 160 | bytes 1280 | tf_op jit(solution)/shard_map/psum | solution.py:59
  103.1 1.0 subtract_multiply_fusion
  104.1 0.6 broadcast_multiply_fusion.1
  (8 shorter events, 0.2 us)
Async XLA Ops:
  0.6 9.6 %copy-start = (f32[160,1024]{1,0:T(8,128)S(1)}, f32[160,1024]{1,0:T(8,128)}, u32[]{:S(2)}) copy-start(f32[160,1024]{1,0:T(8,128)} %param.4) | copy-start | bytes 1966084
  10.3 0.9 copy-start.1
  23.0 12.9 %collective-permute-start = (bf16[160,1280]{1,0:T(8,128)(2,1)S(1)}, bf16[160,1280]{1,0:T(8,128)(2,1)S(1)}, u32[]{:S(2)}, u32[]{:S(2)}) collective-permute-start(bf16[160,1280]{1,0:T(8,128)(2,1)S(1)} %get-tuple-element.98), channel_id=1, source_target_pairs={{12,0},{0,4},{4,8},{8,12},{13,1},{1,5},{5,9},{9,13},{14,2},{2,6},{... | collective-permute-start | bytes 1228808 | tf_op jit(solution)/shard_map/while/body/eval_jaxpr/ppermute | solution.py:15
  47.8 12.8 %collective-permute-start = (bf16[160,1280]{1,0:T(8,128)(2,1)S(1)}, bf16[160,1280]{1,0:T(8,128)(2,1)S(1)}, u32[]{:S(2)}, u32[]{:S(2)}) collective-permute-start(bf16[160,1280]{1,0:T(8,128)(2,1)S(1)} %get-tuple-element.98), channel_id=1, source_target_pairs={{12,0},{0,4},{4,8},{8,12},{13,1},{1,5},{5,9},{9,13},{14,2},{2,6},{... | collective-permute-start | bytes 1228808 | tf_op jit(solution)/shard_map/while/body/eval_jaxpr/ppermute | solution.py:15
  72.3 12.9 %collective-permute-start = (bf16[160,1280]{1,0:T(8,128)(2,1)S(1)}, bf16[160,1280]{1,0:T(8,128)(2,1)S(1)}, u32[]{:S(2)}, u32[]{:S(2)}) collective-permute-start(bf16[160,1280]{1,0:T(8,128)(2,1)S(1)} %get-tuple-element.98), channel_id=1, source_target_pairs={{12,0},{0,4},{4,8},{8,12},{13,1},{1,5},{5,9},{9,13},{14,2},{2,6},{... | collective-permute-start | bytes 1228808 | tf_op jit(solution)/shard_map/while/body/eval_jaxpr/ppermute | solution.py:15
where the time goes:
time: 105 us
  blocking collectives  58.1 us (55%)
  waiting for transfers between devices  36.5 us (35%)
  other arithmetic  3.7 us (4%)
  matrix products  2.71 us (3%)
  starting transfers between devices  1.96 us (2%)
    psum x4, blocking collectives, absorb(): lax.psum((student_term - teacher_term).astype(jnp.bfloat16), 'feat')  43.8 us
    ppermute x3, waiting for transfers between devices, shifted(): return lax.ppermute(block, axis, route)  36.5 us
    psum x1, blocking collectives, on_device(): squares = lax.psum(jnp.sum(student * student, axis=1), 'feat')  8.34 us
    psum x1, blocking collectives, on_device(): radial = lax.psum(jnp.sum(pulled * unit, axis=1), 'feat')  5.89 us
  transfers between devices with their start and end apart: 3, of which 3 were waited for; matrix products, arithmetic and copies ran while one was open for 0% of the time, Pallas kernels for 0%

commit v1 on v0

v1 whole, which is shorter than its diff:
```python
import functools

import jax
import jax.numpy as jnp
from jax import lax
from jax.experimental import pallas as pl
from jax.experimental.pallas import tpu as pltpu
from jax.sharding import PartitionSpec as P

D = 4096
EPSILON = 1e-06
ROWS_LIMIT = 8
LAST = (((1,), (1,)), ((), ()))
FIRST = (((0,), (0,)), ((), ()))
F32 = jnp.float32
BF16 = jnp.bfloat16
MESH = pl.DeviceIdType.MESH


def shifted(block, axis, distance):
    devices = range(lax.axis_size(axis))
    route = [((i - distance) % len(devices), i) for i in devices]
    return lax.ppermute(block, axis, route)


def ring(student, teacher):
    cycle = lax.axis_size("rows")
    rows_here = student.shape[0]
    width = student.shape[1]
    embeds = rows_here * cycle
    squares = lax.psum(jnp.sum(student * student, axis=1), "feat")
    scaling = lax.rsqrt(squares + EPSILON)
    unit = student * scaling[:, None]
    unit_half = unit.astype(BF16)
    packed = jnp.concatenate([unit_half, teacher], axis=1)

    def absorb(carry, visitor):
        losses, pulled = carry
        other_unit = visitor[:, :width]
        other_teacher = visitor[:, width:]
        student_term = lax.dot_general(
            unit_half, other_unit, LAST, preferred_element_type=F32
        )
        teacher_term = lax.dot_general(
            teacher, other_teacher, LAST, preferred_element_type=F32
        )
        differ = lax.psum((student_term - teacher_term).astype(BF16), "feat").astype(F32)
        losses = losses + jnp.sum(differ * differ, axis=1)
        pulled = pulled + jnp.dot(
            differ.astype(BF16), other_unit, preferred_element_type=F32
        )
        return (losses, pulled)

    carry = (jnp.zeros((rows_here,), F32), jnp.zeros((rows_here, width), F32))
    carry = absorb(carry, packed)

    def turn(step, state):
        inner, visitor = state
        visitor = shifted(visitor, "rows", 1)
        return (absorb(inner, visitor), visitor)

    carry, visitor = lax.fori_loop(0, cycle - 1, turn, (carry, packed))
    losses, pulled = carry
    radial = lax.psum(jnp.sum(pulled * unit, axis=1), "feat")
    factor = 4.0 * D / embeds
    student_grad = factor * scaling[:, None] * (pulled - radial[:, None] * unit)
    return (D / embeds * losses, student_grad)


def kernel(
    R, F, C, x_ref, t_ref, loss_ref, g_ref,
    U, T, SQ, CX, TX, rad_ref,
    us, ur, ts, tr, qs, qr, cs, cr, xs, xr,
):
    z = lax.axis_index("rows")
    f = lax.axis_index("feat")
    n, w = x_ref.shape
    rc = n // C
    not_low = z > 0
    not_high = z < R - 1

    bar = pltpu.get_barrier_semaphore()
    for p in range(1, F):
        pl.semaphore_signal(
            bar, inc=1, device_id={"feat": lax.rem(f + p, F)}, device_id_type=MESH
        )

    @pl.when(not_low)
    def _():
        pl.semaphore_signal(bar, inc=1, device_id={"rows": z - 1}, device_id_type=MESH)

    @pl.when(not_high)
    def _():
        pl.semaphore_signal(bar, inc=1, device_id={"rows": z + 1}, device_id_type=MESH)

    eye = lax.broadcasted_iota(jnp.int32, (n, n), 0) == lax.broadcasted_iota(
        jnp.int32, (n, n), 1
    )

    def to_row(column):
        return jnp.sum(jnp.where(eye, column, 0.0), axis=0, keepdims=True)

    def to_column(row):
        return jnp.sum(jnp.where(eye, row, 0.0), axis=1, keepdims=True)

    x = x_ref[...]
    SQ[f] = jnp.broadcast_to(to_row(jnp.sum(x * x, axis=1, keepdims=True)), (8, n))
    T[z] = t_ref[...]
    pl.semaphore_wait(
        bar, F - 1 + not_low.astype(jnp.int32) + not_high.astype(jnp.int32)
    )

    def across(buf, index, send, recv, p, mine):
        owner = f if mine else lax.rem(f + F - p, F)
        ref = buf.at[(owner,) + index]
        return pltpu.make_async_remote_copy(
            src_ref=ref, dst_ref=ref,
            send_sem=send.at[index + (p - 1,)], recv_sem=recv.at[index + (p - 1,)],
            device_id={"feat": lax.rem(f + p, F)}, device_id_type=MESH,
        )

    def spread(buf, index, send, recv):
        for p in range(1, F):
            across(buf, index, send, recv, p, True).start()

    def collect(buf, index, send, recv):
        for p in range(1, F):
            across(buf, index, send, recv, p, False).wait_recv()

    def drained(buf, index, send, recv):
        for p in range(1, F):
            across(buf, index, send, recv, p, True).wait_send()

    def along(buf, d, src, place, index, send, recv):
        ref = buf.at[(src,) + place]
        target = lax.rem(z + (1 if d == 0 else R - 1), R)
        return pltpu.make_async_remote_copy(
            src_ref=ref, dst_ref=ref,
            send_sem=send.at[(d,) + index], recv_sem=recv.at[(d,) + index],
            device_id={"rows": target}, device_id_type=MESH,
        )

    def sends(d, k):
        if d == 0:
            return jnp.logical_and(z - k >= 0, not_high), z - k
        return jnp.logical_and(z + k <= R - 1, not_low), z + k

    def arrives(d, k):
        if d == 0:
            return z - 1 - k >= 0, z - 1 - k
        return z + 1 + k <= R - 1, z + 1 + k

    def t_copy(d, k, src):
        return along(T, d, src, (), (k,), ts, tr)

    def u_copy(d, k, c, src):
        return along(U, d, src, (c,), (k, c), us, ur)

    spread(SQ, (), qs, qr)
    for d in range(2):
        here, src = sends(d, 0)

        @pl.when(here)
        def _(d=d, src=src):
            t_copy(d, 0, src).start()

    collect(SQ, (), qs, qr)
    squares = SQ[0]
    for g in range(1, F):
        squares = squares + SQ[g]
    scaling = to_column(lax.rsqrt(squares[:1] + EPSILON))
    U[z] = (x_ref[...] * scaling).astype(BF16).reshape(C, rc, w)
    for c in range(C):
        for d in range(2):
            here, src = sends(d, 0)

            @pl.when(here)
            def _(d=d, c=c, src=src):
                u_copy(d, 0, c, src).start()

    def teach(src):
        TX[f, src] = lax.dot_general(
            T[src], t_ref[...], LAST, preferred_element_type=F32
        ).astype(BF16)
        spread(TX, (src,), xs, xr)

    def study(src, c):
        CX[f, src, c] = lax.dot_general(
            U[src, c], U[z].reshape(n, w), LAST, preferred_element_type=F32
        ).astype(BF16)
        spread(CX, (src, c), cs, cr)

    def finish(src, first=False):
        collect(TX, (src,), xs, xr)
        teacher = TX[0, src].astype(F32)
        for g in range(1, F):
            teacher = teacher + TX[g, src].astype(F32)
        for c in range(C):
            collect(CX, (src, c), cs, cr)
        cosine = CX[0, src].astype(F32)
        for g in range(1, F):
            cosine = cosine + CX[g, src].astype(F32)
        cosine = cosine.reshape(n, n)
        differ = cosine - teacher
        half = differ.astype(BF16)
        loss = jnp.sum(differ * differ, axis=0, keepdims=True)
        radial = jnp.sum(half.astype(F32) * cosine, axis=0, keepdims=True)
        pulled = lax.dot_general(
            half, U[src].reshape(n, w), FIRST, preferred_element_type=F32
        )
        if first:
            loss_ref[...] = loss
            rad_ref[...] = radial
            g_ref[...] = pulled
        else:
            loss_ref[...] += loss
            rad_ref[...] += radial
            g_ref[...] += pulled

    teach(z)
    for c in range(C):
        study(z, c)

    for k in range(R - 1):
        for d in range(2):
            here, src = arrives(d, k)

            @pl.when(here)
            def _(d=d, k=k, src=src):
                t_copy(d, k, src).wait_recv()
                if k < R - 2:
                    @pl.when(sends(d, k + 1)[0])
                    def _():
                        t_copy(d, k + 1, src).start()
                teach(src)

        if k == 0:
            finish(z, True)
        else:
            for d in range(2):
                here, src = arrives(d, k - 1)

                @pl.when(here)
                def _(src=src):
                    finish(src)

        for c in range(C):
            for d in range(2):
                here, src = arrives(d, k)

                @pl.when(here)
                def _(d=d, k=k, c=c, src=src):
                    u_copy(d, k, c, src).wait_recv()
                    if k < R - 2:
                        @pl.when(sends(d, k + 1)[0])
                        def _():
                            u_copy(d, k + 1, c, src).start()
                    study(src, c)

    for d in range(2):
        here, src = arrives(d, R - 2)

        @pl.when(here)
        def _(src=src):
            finish(src)

    factor = 4.0 * D / (n * R)
    loss_ref[...] = (D / (n * R)) * loss_ref[...]
    radial = to_column(rad_ref[...])
    g_ref[...] = (factor * scaling) * (g_ref[...] - (radial * scaling) * x_ref[...])

    drained(SQ, (), qs, qr)
    for src in range(R):
        drained(TX, (src,), xs, xr)
        for c in range(C):
            drained(CX, (src, c), cs, cr)
    for k in range(R - 1):
        for d in range(2):
            here, src = sends(d, k)

            @pl.when(here)
            def _(d=d, k=k, src=src):
                t_copy(d, k, src).wait_send()
                for c in range(C):
                    u_copy(d, k, c, src).wait_send()


def fused(R, F, student, teacher):
    n, w = student.shape
    wt = teacher.shape[1]
    C = 2 if n % 32 == 0 else 1
    dma = pltpu.SemaphoreType.DMA
    vmem = pl.BlockSpec(memory_space=pltpu.VMEM)
    loss, grad = pl.pallas_call(
        functools.partial(kernel, R, F, C),
        out_shape=(
            jax.ShapeDtypeStruct((1, n), F32),
            jax.ShapeDtypeStruct((n, w), F32),
        ),
        in_specs=[vmem, vmem],
        out_specs=(vmem, vmem),
        scratch_shapes=[
            pltpu.VMEM((R, C, n // C, w), BF16),
            pltpu.VMEM((R, n, wt), BF16),
            pltpu.VMEM((F, 8, n), F32),
            pltpu.VMEM((F, R, C, n // C, n), BF16),
            pltpu.VMEM((F, R, n, n), BF16),
            pltpu.VMEM((1, n), F32),
            dma((2, R - 1, C)), dma((2, R - 1, C)),
            dma((2, R - 1)), dma((2, R - 1)),
            dma((F - 1,)), dma((F - 1,)),
            dma((R, C, F - 1)), dma((R, C, F - 1)),
            dma((R, F - 1)), dma((R, F - 1)),
        ],
        compiler_params=pltpu.CompilerParams(
            collective_id=0, has_side_effects=True, vmem_limit_bytes=40 * 2**20
        ),
    )(student, teacher)
    return loss.reshape(n), grad


def solution(mesh):
    R, F = mesh.shape["rows"], mesh.shape["feat"]
    body = functools.partial(fused, R, F) if 2 <= R <= ROWS_LIMIT and F > 1 else ring
    in_specs = (P(("groups", "rows"), "feat"), P(("groups", "rows"), "feat"))
    out_specs = (P(("groups", "rows")), P(("groups", "rows"), "feat"))
    return jax.shard_map(
        body, mesh=mesh, in_specs=in_specs, out_specs=out_specs, check_vma=False
    )
```

time: 105 us -> 48.6 us (0.46)
  blocking collectives: 58.1 us -> 0 us
  Pallas kernels: 0 us -> 44.4 us
  waiting for transfers between devices: 36.5 us -> 0 us
  other arithmetic: 3.7 us -> 0 us
  matrix products: 2.71 us -> 0 us
  local copies, waits for them, and re-layouts: 0.87 us -> 3.37 us
  starting transfers between devices: 1.96 us -> 0 us
    psum x6 -> x0, blocking collectives: 58.1 us -> none  [the longest x4 43.8 us: absorb(): lax.psum((student_term - teacher_term).astype(jnp.bfloat16), 'feat')]
    pallas_call x0 -> x1, Pallas kernels: none -> 44.4 us  [fused(): pl.pallas_call(functools.partial(kernel, R, F, C), out_shape=(jax.ShapeDt...]
    ppermute x3 -> x0, waiting for transfers between devices: 36.5 us -> none  [shifted(): return lax.ppermute(block, axis, route)]
    dot_general x12 -> x0, matrix products: 2.71 us -> none  [the longest x4 1.07 us: absorb(): lax.dot_general(unit_half, other_unit, contract, preferred_element_type=j...]
    unnamed x4 -> x6, local copies, waits for them, and re-layouts: 0.78 us -> 3.37 us
    ppermute x3 -> x0, starting transfers between devices: 1.96 us -> none  [shifted(): return lax.ppermute(block, axis, route)]
    reduce_sum x6 -> x0, other arithmetic: 1.95 us -> none  [the longest x1 1.28 us: on_device(): squares = lax.psum(jnp.sum(student * student, axis=1), 'feat')]
    mul x3 -> x0, other arithmetic: 1.59 us -> none  [the longest x2 1.03 us: on_device(): student_grad = factor * scaling[:, None] * (pulled - radial[:, None] * unit)]
  transfers between devices with their start and end apart: 3 -> 0, of which waited for: 3 -> 0; matrix products, arithmetic and copies ran while one was open for 0% -> 0% of each run, Pallas kernels for 0% -> 0%
where the time goes in v1:
time: 48.6 us; the launch traced here: 48.4 us
  Pallas kernels  44.4 us (91%)
  local copies, waits for them, and re-layouts  3.37 us (7%)
  between operations  0.65 us (1%)
    pallas_call x1, Pallas kernels, fused(): pl.pallas_call(functools.partial(kernel, R, F, C), out_shape=(jax.ShapeDt...  44.4 us
    unnamed x6, local copies, waits for them, and re-layouts  3.37 us

profile of v1, /device:TPU:0, one launch (start us, length us, event | category | flops | bytes accessed | tf_op | source)
XLA Modules:
  0.0 48.4 jit_solution(17393573163813944361)
XLA Ops:
  0.6 0.0 copy-start
  0.6 1.1 %copy-done = f32[160,1024]{1,0:T(8,128)S(1)} copy-done((f32[160,1024]{1,0:T(8,128)S(1)}, f32[160,1024]{1,0:T(8,128)}, u32[]{:S(2)}) %copy-start) | copy-done | bytes 655384
  1.7 0.0 copy-start.1
  1.7 0.9 %copy-done.1 = bf16[160,256]{1,0:T(8,128)(2,1)S(1)} copy-done((bf16[160,256]{1,0:T(8,128)(2,1)S(1)}, bf16[160,256]{1,0:T(8,128)(2,1)}, u32[]{:S(2)}) %copy-start.1) | copy-done | bytes 81944
  2.6 44.4 %shard_map.41 = (f32[1,160]{1,0:T(1,128)S(1)}, f32[160,1024]{1,0:T(8,128)S(1)}) custom-call(f32[160,1024]{1,0:T(8,128)S(1)} %copy-done, bf16[160,256]{1,0:T(8,128)(2,1)S(1)} %copy-done.1), custom_call_target="tpu_custom_call" | custom-call | tf_op jit(solution)/shard_map/pallas_call | solution.py:294
  47.0 0.6 %copy.6 = f32[160]{0:T(256)} copy(f32[160]{0:T(256)S(1)} %bitcast.1) | data formatting | bytes 1280
  47.6 0.8 %copy.7 = f32[160,1024]{1,0:T(8,128)} copy(f32[160,1024]{1,0:T(8,128)S(1)} %get-tuple-element.9) | data formatting | bytes 1310720
Async XLA Ops:
  0.6 1.1 %copy-start = (f32[160,1024]{1,0:T(8,128)S(1)}, f32[160,1024]{1,0:T(8,128)}, u32[]{:S(2)}) copy-start(f32[160,1024]{1,0:T(8,128)} %x_ref.1) | copy-start | bytes 1966084
  1.7 0.9 %copy-start.1 = (bf16[160,256]{1,0:T(8,128)(2,1)S(1)}, bf16[160,256]{1,0:T(8,128)(2,1)}, u32[]{:S(2)}) copy-start(bf16[160,256]{1,0:T(8,128)(2,1)} %t_ref.1) | copy-start | bytes 245764

commit v2 on v1

v2 whole, which is shorter than its diff:
```python
import functools

import jax
import jax.numpy as jnp
from jax import lax
from jax.experimental import pallas as pl
from jax.experimental.pallas import tpu as pltpu
from jax.sharding import PartitionSpec as P

D = 4096
EPSILON = 1e-06
ROWS_LIMIT = 8
LAST = (((1,), (1,)), ((), ()))
FIRST = (((0,), (0,)), ((), ()))
F32 = jnp.float32
BF16 = jnp.bfloat16
MESH = pl.DeviceIdType.MESH


def shifted(block, axis, distance):
    devices = range(lax.axis_size(axis))
    route = [((i - distance) % len(devices), i) for i in devices]
    return lax.ppermute(block, axis, route)


def ring(student, teacher):
    cycle = lax.axis_size("rows")
    rows_here = student.shape[0]
    width = student.shape[1]
    embeds = rows_here * cycle
    squares = lax.psum(jnp.sum(student * student, axis=1), "feat")
    scaling = lax.rsqrt(squares + EPSILON)
    unit = student * scaling[:, None]
    unit_half = unit.astype(BF16)
    packed = jnp.concatenate([unit_half, teacher], axis=1)

    def absorb(carry, visitor):
        losses, pulled = carry
        other_unit = visitor[:, :width]
        other_teacher = visitor[:, width:]
        student_term = lax.dot_general(
            unit_half, other_unit, LAST, preferred_element_type=F32
        )
        teacher_term = lax.dot_general(
            teacher, other_teacher, LAST, preferred_element_type=F32
        )
        differ = lax.psum((student_term - teacher_term).astype(BF16), "feat").astype(F32)
        losses = losses + jnp.sum(differ * differ, axis=1)
        pulled = pulled + jnp.dot(
            differ.astype(BF16), other_unit, preferred_element_type=F32
        )
        return (losses, pulled)

    carry = (jnp.zeros((rows_here,), F32), jnp.zeros((rows_here, width), F32))
    carry = absorb(carry, packed)

    def turn(step, state):
        inner, visitor = state
        visitor = shifted(visitor, "rows", 1)
        return (absorb(inner, visitor), visitor)

    carry, visitor = lax.fori_loop(0, cycle - 1, turn, (carry, packed))
    losses, pulled = carry
    radial = lax.psum(jnp.sum(pulled * unit, axis=1), "feat")
    factor = 4.0 * D / embeds
    student_grad = factor * scaling[:, None] * (pulled - radial[:, None] * unit)
    return (D / embeds * losses, student_grad)


def kernel(
    R, F, C, x_hbm, t_hbm, loss_ref, g_ref,
    x_ref, t_ref, U, T, SQ, TP, TQ, TX, CP, CQ, CX, DX, rad_ref,
    ins, us, ur, ts, tr, qs, qr, tps, tpr, txs, txr, cps, cpr, cxs, cxr, dxs, dxr,
):
    z = lax.axis_index("rows")
    f = lax.axis_index("feat")
    core = lax.rem(f, 2)
    chip = lax.div(f, 2)
    n, w = x_ref.shape
    h = n // 2
    rc = n // C
    not_low = z > 0
    not_high = z < R - 1

    bar = pltpu.get_barrier_semaphore()
    for p in range(1, F):
        pl.semaphore_signal(
            bar, inc=1, device_id={"feat": lax.rem(f + p, F)}, device_id_type=MESH
        )

    @pl.when(not_low)
    def _():
        pl.semaphore_signal(bar, inc=1, device_id={"rows": z - 1}, device_id_type=MESH)

    @pl.when(not_high)
    def _():
        pl.semaphore_signal(bar, inc=1, device_id={"rows": z + 1}, device_id_type=MESH)

    x_in = pltpu.make_async_copy(x_hbm, x_ref, ins.at[0])
    t_in = pltpu.make_async_copy(t_hbm, t_ref, ins.at[1])
    x_in.start()
    t_in.start()

    eye = lax.broadcasted_iota(jnp.int32, (n, n), 0) == lax.broadcasted_iota(
        jnp.int32, (n, n), 1
    )

    def to_row(column):
        return jnp.sum(jnp.where(eye, column, 0.0), axis=0, keepdims=True)

    def to_column(row):
        return jnp.sum(jnp.where(eye, row, 0.0), axis=1, keepdims=True)

    x_in.wait()
    x = x_ref[...]
    SQ[f] = jnp.broadcast_to(to_row(jnp.sum(x * x, axis=1, keepdims=True)), (8, n))
    t_in.wait()
    T[z] = t_ref[...]
    pl.semaphore_wait(
        bar, F - 1 + not_low.astype(jnp.int32) + not_high.astype(jnp.int32)
    )

    def remote(src, dst, send, recv, device):
        return pltpu.make_async_remote_copy(
            src_ref=src, dst_ref=dst, send_sem=send, recv_sem=recv,
            device_id=device, device_id_type=MESH,
        )

    def across(entry, index, send, recv, p, mine):
        ref = entry(f if mine else lax.rem(f + F - p, F))
        return remote(
            ref, ref, send.at[index + (p - 1,)], recv.at[index + (p - 1,)],
            {"feat": lax.rem(f + p, F)},
        )

    def spread(entry, index, send, recv):
        for p in range(1, F):
            across(entry, index, send, recv, p, True).start()

    def collect(entry, index, send, recv):
        for p in range(1, F):
            across(entry, index, send, recv, p, False).wait_recv()

    def drained(entry, index, send, recv):
        for p in range(1, F):
            across(entry, index, send, recv, p, True).wait_send()

    def halves(buf, src):
        return lambda g: buf.at[lax.div(g, 2), src, lax.rem(g, 2)]

    def sibling(part, other, src, send, recv):
        return remote(
            part.at[src, 1 - core], other.at[src], send.at[src], recv.at[src],
            {"feat": f + 1 - 2 * core},
        )

    def along(buf, d, src, place, index, send, recv):
        ref = buf.at[(src,) + place]
        target = lax.rem(z + (1 if d == 0 else R - 1), R)
        return remote(
            ref, ref, send.at[(d,) + index], recv.at[(d,) + index], {"rows": target}
        )

    def sends(d, k):
        if d == 0:
            return jnp.logical_and(z - k >= 0, not_high), z - k
        return jnp.logical_and(z + k <= R - 1, not_low), z + k

    def arrives(d, k):
        if d == 0:
            return z - 1 - k >= 0, z - 1 - k
        return z + 1 + k <= R - 1, z + 1 + k

    def each(k, act):
        for d in range(2):
            here, src = arrives(d, k)

            @pl.when(here)
            def _(d=d, src=src):
                act(d, src)

    def t_copy(d, k, src):
        return along(T, d, src, (), (k,), ts, tr)

    def u_copy(d, k, c, src):
        return along(U, d, src, (c,), (k, c), us, ur)

    squares_of = lambda g: SQ.at[g]
    spread(squares_of, (), qs, qr)
    for d in range(2):
        here, src = sends(d, 0)

        @pl.when(here)
        def _(d=d, src=src):
            t_copy(d, 0, src).start()

    collect(squares_of, (), qs, qr)
    squares = SQ[0]
    for g in range(1, F):
        squares = squares + SQ[g]
    scaling = to_column(lax.rsqrt(squares[:1] + EPSILON))
    U[z] = (x_ref[...] * scaling).astype(BF16).reshape(C, rc, w)
    for c in range(C):
        for d in range(2):
            here, src = sends(d, 0)

            @pl.when(here)
            def _(d=d, c=c, src=src):
                u_copy(d, 0, c, src).start()

    def teach(src):
        TP[src] = lax.dot_general(
            T[src], t_ref[...], LAST, preferred_element_type=F32
        ).astype(BF16).reshape(2, h, n)
        sibling(TP, TQ, src, tps, tpr).start()

    def teach_on(src):
        sibling(TP, TQ, src, tps, tpr).wait_recv()
        TX[chip, src, core] = (TP[src, core].astype(F32) + TQ[src].astype(F32)).astype(BF16)
        spread(halves(TX, src), (src,), txs, txr)

    def gram(src, c):
        return lax.dot_general(
            U[src, c], U[z].reshape(n, w), LAST, preferred_element_type=F32
        ).astype(BF16)

    def study(src, c):
        CP[src, c] = gram(src, c)
        if c == C - 1:
            sibling(CP, CQ, src, cps, cpr).start()

    def study_on(src):
        sibling(CP, CQ, src, cps, cpr).wait_recv()
        CX[chip, src, core] = (CP[src, core].astype(F32) + CQ[src].astype(F32)).astype(BF16)
        spread(halves(CX, src), (src,), cxs, cxr)

    def direct_of(c):
        return lambda g: DX.at[g, c]

    def study_direct(src, c):
        DX[f, c] = gram(src, c)
        spread(direct_of(c), (c,), dxs, dxr)

    def finish(src, first=False, direct=False):
        collect(halves(TX, src), (src,), txs, txr)
        teacher = TX[0, src].astype(F32) + TX[1, src].astype(F32)
        if direct:
            for c in range(C):
                collect(direct_of(c), (c,), dxs, dxr)
            cosine = DX[0].astype(F32)
            for g in range(1, F):
                cosine = cosine + DX[g].astype(F32)
        else:
            collect(halves(CX, src), (src,), cxs, cxr)
            cosine = CX[0, src].astype(F32) + CX[1, src].astype(F32)
        cosine = cosine.reshape(n, n)
        differ = cosine - teacher.reshape(n, n)
        half = differ.astype(BF16)
        loss = jnp.sum(differ * differ, axis=0, keepdims=True)
        radial = jnp.sum(half.astype(F32) * cosine, axis=0, keepdims=True)
        pulled = lax.dot_general(
            half, U[src].reshape(n, w), FIRST, preferred_element_type=F32
        )
        if first:
            loss_ref[...] = loss
            rad_ref[...] = radial
            g_ref[...] = pulled
        else:
            loss_ref[...] += loss
            rad_ref[...] += radial
            g_ref[...] += pulled

    teach(z)
    for c in range(C):
        study(z, c)
    teach_on(z)
    study_on(z)

    for k in range(R - 1):
        last = k == R - 2

        def t_step(d, src, k=k):
            t_copy(d, k, src).wait_recv()
            if k < R - 2:
                @pl.when(sends(d, k + 1)[0])
                def _():
                    t_copy(d, k + 1, src).start()
            teach(src)

        each(k, t_step)
        if k > 0:
            each(k - 1, lambda d, src: study_on(src))
        each(k, lambda d, src: teach_on(src))
        for c in range(C):

            def u_step(d, src, k=k, c=c, last=last):
                u_copy(d, k, c, src).wait_recv()
                if not last:
                    @pl.when(sends(d, k + 1)[0])
                    def _():
                        u_copy(d, k + 1, c, src).start()
                if last:
                    study_direct(src, c)
                else:
                    study(src, c)

            each(k, u_step)
            if c == 0:
                if k == 0:
                    finish(z, first=True)
                else:
                    each(k - 1, lambda d, src: finish(src))

    each(R - 2, lambda d, src: finish(src, direct=True))

    factor = 4.0 * D / (n * R)
    loss_ref[...] = (D / (n * R)) * loss_ref[...]
    radial = to_column(rad_ref[...])
    g_ref[...] = (factor * scaling) * (g_ref[...] - (radial * scaling) * x_ref[...])

    drained(squares_of, (), qs, qr)

    def t_drained(d, src):
        sibling(TP, TQ, src, tps, tpr).wait_send()
        drained(halves(TX, src), (src,), txs, txr)

    def c_drained(d, src):
        sibling(CP, CQ, src, cps, cpr).wait_send()
        drained(halves(CX, src), (src,), cxs, cxr)

    t_drained(0, z)
    c_drained(0, z)
    for k in range(R - 1):
        each(k, t_drained)
        if k < R - 2:
            each(k, c_drained)
        else:
            each(k, lambda d, src: [drained(direct_of(c), (c,), dxs, dxr) for c in range(C)])
        for d in range(2):
            here, src = sends(d, k)

            @pl.when(here)
            def _(d=d, k=k, src=src):
                t_copy(d, k, src).wait_send()
                for c in range(C):
                    u_copy(d, k, c, src).wait_send()


def fused(R, F, student, teacher):
    n, w = student.shape
    wt = teacher.shape[1]
    C = 2
    h = n // 2
    dma = pltpu.SemaphoreType.DMA
    vmem = pl.BlockSpec(memory_space=pltpu.VMEM)
    hbm = pl.BlockSpec(memory_space=pltpu.HBM)
    loss, grad = pl.pallas_call(
        functools.partial(kernel, R, F, C),
        out_shape=(
            jax.ShapeDtypeStruct((1, n), F32),
            jax.ShapeDtypeStruct((n, w), F32),
        ),
        in_specs=[hbm, hbm],
        out_specs=(vmem, vmem),
        scratch_shapes=[
            pltpu.VMEM((n, w), F32),
            pltpu.VMEM((n, wt), BF16),
            pltpu.VMEM((R, C, n // C, w), BF16),
            pltpu.VMEM((R, n, wt), BF16),
            pltpu.VMEM((F, 8, n), F32),
            pltpu.VMEM((R, 2, h, n), BF16),
            pltpu.VMEM((R, h, n), BF16),
            pltpu.VMEM((2, R, 2, h, n), BF16),
            pltpu.VMEM((R, 2, h, n), BF16),
            pltpu.VMEM((R, h, n), BF16),
            pltpu.VMEM((2, R, 2, h, n), BF16),
            pltpu.VMEM((F, C, n // C, n), BF16),
            pltpu.VMEM((1, n), F32),
            dma((2,)),
            dma((2, R - 1, C)), dma((2, R - 1, C)),
            dma((2, R - 1)), dma((2, R - 1)),
            dma((F - 1,)), dma((F - 1,)),
            dma((R,)), dma((R,)), dma((R, F - 1)), dma((R, F - 1)),
            dma((R,)), dma((R,)), dma((R, F - 1)), dma((R, F - 1)),
            dma((C, F - 1)), dma((C, F - 1)),
        ],
        compiler_params=pltpu.CompilerParams(
            collective_id=0, has_side_effects=True, vmem_limit_bytes=48 * 2**20
        ),
    )(student, teacher)
    return loss.reshape(n), grad


def solution(mesh):
    R, F = mesh.shape["rows"], mesh.shape["feat"]
    body = functools.partial(fused, R, F) if 2 <= R <= ROWS_LIMIT and F == 4 else ring
    in_specs = (P(("groups", "rows"), "feat"), P(("groups", "rows"), "feat"))
    out_specs = (P(("groups", "rows")), P(("groups", "rows"), "feat"))
    return jax.shard_map(
        body, mesh=mesh, in_specs=in_specs, out_specs=out_specs, check_vma=False
    )
```

time: 48.6 us -> 42.1 us (0.87)
  Pallas kernels: 44.4 us -> 37.8 us
    pallas_call x1, Pallas kernels: 44.4 us -> 37.8 us  [fused(): pl.pallas_call(functools.partial(kernel, R, F, C), out_shape=(jax.ShapeDt...]
where the time goes in v2:
time: 42.1 us; the launch traced here: 41.9 us
  Pallas kernels  37.8 us (90%)
  local copies, waits for them, and re-layouts  3.37 us (8%)
  between operations  0.65 us (2%)
    pallas_call x1, Pallas kernels, fused(): pl.pallas_call(functools.partial(kernel, R, F, C), out_shape=(jax.ShapeDt...  37.8 us
    unnamed x6, local copies, waits for them, and re-layouts  3.37 us

profile of v2, /device:TPU:0, one launch (start us, length us, event | category | flops | bytes accessed | tf_op | source)
XLA Modules:
  0.0 41.9 jit_solution(12342412528402101908)
XLA Ops:
  0.6 0.0 copy-start
  0.6 1.1 %copy-done = f32[160,1024]{1,0:T(8,128)S(1)} copy-done((f32[160,1024]{1,0:T(8,128)S(1)}, f32[160,1024]{1,0:T(8,128)}, u32[]{:S(2)}) %copy-start) | copy-done | bytes 655384
  1.7 0.0 copy-start.1
  1.7 0.9 %copy-done.1 = bf16[160,256]{1,0:T(8,128)(2,1)S(1)} copy-done((bf16[160,256]{1,0:T(8,128)(2,1)S(1)}, bf16[160,256]{1,0:T(8,128)(2,1)}, u32[]{:S(2)}) %copy-start.1) | copy-done | bytes 81944
  2.6 37.8 %shard_map.41 = (f32[1,160]{1,0:T(1,128)S(1)}, f32[160,1024]{1,0:T(8,128)S(1)}) custom-call(f32[160,1024]{1,0:T(8,128)S(1)} %copy-done, bf16[160,256]{1,0:T(8,128)(2,1)S(1)} %copy-done.1), custom_call_target="tpu_custom_call" | custom-call | tf_op jit(solution)/shard_map/pallas_call | solution.py:357
  40.5 0.6 %copy.6 = f32[160]{0:T(256)} copy(f32[160]{0:T(256)S(1)} %bitcast.1) | data formatting | bytes 1280
  41.0 0.8 %copy.7 = f32[160,1024]{1,0:T(8,128)} copy(f32[160,1024]{1,0:T(8,128)S(1)} %get-tuple-element.9) | data formatting | bytes 1310720
Async XLA Ops:
  0.6 1.1 %copy-start = (f32[160,1024]{1,0:T(8,128)S(1)}, f32[160,1024]{1,0:T(8,128)}, u32[]{:S(2)}) copy-start(f32[160,1024]{1,0:T(8,128)} %x_hbm.1) | copy-start | bytes 1966084
  1.7 0.9 %copy-start.1 = (bf16[160,256]{1,0:T(8,128)(2,1)S(1)}, bf16[160,256]{1,0:T(8,128)(2,1)}, u32[]{:S(2)}) copy-start(bf16[160,256]{1,0:T(8,128)(2,1)} %t_hbm.1) | copy-start | bytes 245764

commit v3 on v2

--- a/solution.py
+++ b/solution.py
@@ -69,8 +69,8 @@
 
 def kernel(
     R, F, C, x_hbm, t_hbm, loss_ref, g_ref,
-    x_ref, t_ref, U, T, SQ, TP, TQ, TX, CP, CQ, CX, DX, rad_ref,
-    ins, us, ur, ts, tr, qs, qr, tps, tpr, txs, txr, cps, cpr, cxs, cxr, dxs, dxr,
+    x_ref, t_ref, U, T, SQ, TP, TQ, TX, CP, CQ, CX, DX, KP, RX, rad_ref,
+    ins, us, ur, ts, tr, qs, qr, tps, tpr, txs, txr, cps, cpr, cxs, cxr, dxs, dxr, rs, rr,
 ):
     z = lax.axis_index("rows")
     f = lax.axis_index("feat")
@@ -222,10 +222,15 @@
     def gram(src, c):
         return lax.dot_general(
             U[src, c], U[z].reshape(n, w), LAST, preferred_element_type=F32
-        ).astype(BF16)
+        )
 
     def study(src, c):
-        CP[src, c] = gram(src, c)
+        cosine = gram(src, c)
+        KP[src, c] = cosine
+        teacher = lax.dot_general(
+            T[src].reshape(C, rc, -1)[c], t_ref[...], LAST, preferred_element_type=F32
+        )
+        CP[src, c] = (cosine - teacher).astype(BF16)
         if c == C - 1:
             sibling(CP, CQ, src, cps, cpr).start()
 
@@ -238,23 +243,26 @@
         return lambda g: DX.at[g, c]
 
     def study_direct(src, c):
-        DX[f, c] = gram(src, c)
+        DX[f, c] = gram(src, c).astype(BF16)
         spread(direct_of(c), (c,), dxs, dxr)
 
+    radial_of = lambda g: RX.at[g]
+
     def finish(src, first=False, direct=False):
-        collect(halves(TX, src), (src,), txs, txr)
-        teacher = TX[0, src].astype(F32) + TX[1, src].astype(F32)
         if direct:
+            collect(halves(TX, src), (src,), txs, txr)
+            teacher = TX[0, src].astype(F32) + TX[1, src].astype(F32)
             for c in range(C):
                 collect(direct_of(c), (c,), dxs, dxr)
             cosine = DX[0].astype(F32)
             for g in range(1, F):
                 cosine = cosine + DX[g].astype(F32)
+            cosine = cosine.reshape(n, n)
+            differ = cosine - teacher.reshape(n, n)
         else:
             collect(halves(CX, src), (src,), cxs, cxr)
-            cosine = CX[0, src].astype(F32) + CX[1, src].astype(F32)
-        cosine = cosine.reshape(n, n)
-        differ = cosine - teacher.reshape(n, n)
+            differ = (CX[0, src].astype(F32) + CX[1, src].astype(F32)).reshape(n, n)
+            cosine = KP[src].reshape(n, n)
         half = differ.astype(BF16)
         loss = jnp.sum(differ * differ, axis=0, keepdims=True)
         radial = jnp.sum(half.astype(F32) * cosine, axis=0, keepdims=True)
@@ -263,55 +271,71 @@
         )
         if first:
             loss_ref[...] = loss
-            rad_ref[...] = radial
+            RX[f] = jnp.broadcast_to(radial, (8, n))
+            rad_ref[...] = jnp.zeros_like(radial)
             g_ref[...] = pulled
         else:
             loss_ref[...] += loss
-            rad_ref[...] += radial
+            if direct:
+                rad_ref[...] += radial
+            else:
+                RX[f] += radial
             g_ref[...] += pulled
 
-    teach(z)
     for c in range(C):
         study(z, c)
-    teach_on(z)
     study_on(z)
 
-    for k in range(R - 1):
-        last = k == R - 2
-
-        def t_step(d, src, k=k):
+    def t_step(k):
+        def act(d, src):
             t_copy(d, k, src).wait_recv()
             if k < R - 2:
                 @pl.when(sends(d, k + 1)[0])
                 def _():
                     t_copy(d, k + 1, src).start()
-            teach(src)
-
-        each(k, t_step)
+            else:
+                teach(src)
+
+        each(k, act)
+
+    def u_move(k, c, d, side):
+        here, src = arrives(d, k)
+
+        @pl.when(jnp.logical_and(here, side))
+        def _():
+            u_copy(d, k, c, src).wait_recv()
+            if k < R - 2:
+                @pl.when(sends(d, k + 1)[0])
+                def _():
+                    u_copy(d, k + 1, c, src).start()
+
+    def u_step(k, c):
+        for d in (1, 0):
+            u_move(k, c, d, z < R // 2)
+        for d in (0, 1):
+            u_move(k, c, d, z >= R // 2)
+        each(k, lambda d, src: study(src, c) if k < R - 2 else study_direct(src, c))
+
+    for k in range(R - 1):
+        t_step(k)
         if k > 0:
             each(k - 1, lambda d, src: study_on(src))
-        each(k, lambda d, src: teach_on(src))
-        for c in range(C):
-
-            def u_step(d, src, k=k, c=c, last=last):
-                u_copy(d, k, c, src).wait_recv()
-                if not last:
-                    @pl.when(sends(d, k + 1)[0])
-                    def _():
-                        u_copy(d, k + 1, c, src).start()
-                if last:
-                    study_direct(src, c)
-                else:
-                    study(src, c)
-
-            each(k, u_step)
-            if c == 0:
-                if k == 0:
-                    finish(z, first=True)
-                else:
-                    each(k - 1, lambda d, src: finish(src))
+        u_step(k, 0)
+        if k == 0:
+            finish(z, first=True)
+        else:
+            if k == R - 2:
+                each(k, lambda d, src: teach_on(src))
+            each(k - 1, lambda d, src: finish(src))
+        if k == R - 2:
+            spread(radial_of, (), rs, rr)
+        u_step(k, 1)
 
     each(R - 2, lambda d, src: finish(src, direct=True))
+
+    collect(radial_of, (), rs, rr)
+    for g in range(F):
+        rad_ref[...] += RX[g, :1]
 
     factor = 4.0 * D / (n * R)
     loss_ref[...] = (D / (n * R)) * loss_ref[...]
@@ -319,6 +343,7 @@
     g_ref[...] = (factor * scaling) * (g_ref[...] - (radial * scaling) * x_ref[...])
 
     drained(squares_of, (), qs, qr)
+    drained(radial_of, (), rs, rr)
 
     def t_drained(d, src):
         sibling(TP, TQ, src, tps, tpr).wait_send()
@@ -328,13 +353,12 @@
         sibling(CP, CQ, src, cps, cpr).wait_send()
         drained(halves(CX, src), (src,), cxs, cxr)
 
-    t_drained(0, z)
     c_drained(0, z)
     for k in range(R - 1):
-        each(k, t_drained)
         if k < R - 2:
             each(k, c_drained)
         else:
+            each(k, t_drained)
             each(k, lambda d, src: [drained(direct_of(c), (c,), dxs, dxr) for c in range(C)])
         for d in range(2):
             here, src = sends(d, k)
@@ -375,6 +399,8 @@
             pltpu.VMEM((R, h, n), BF16),
             pltpu.VMEM((2, R, 2, h, n), BF16),
             pltpu.VMEM((F, C, n // C, n), BF16),
+            pltpu.VMEM((R, C, n // C, n), F32),
+            pltpu.VMEM((F, 8, n), F32),
             pltpu.VMEM((1, n), F32),
             dma((2,)),
             dma((2, R - 1, C)), dma((2, R - 1, C)),
@@ -383,17 +409,18 @@
             dma((R,)), dma((R,)), dma((R, F - 1)), dma((R, F - 1)),
             dma((R,)), dma((R,)), dma((R, F - 1)), dma((R, F - 1)),
             dma((C, F - 1)), dma((C, F - 1)),
+            dma((F - 1,)), dma((F - 1,)),
         ],
         compiler_params=pltpu.CompilerParams(
             collective_id=0, has_side_effects=True, vmem_limit_bytes=48 * 2**20
         ),
-    )(student, teacher)
+    )(pltpu.with_memory_space_constraint(student, pltpu.HBM), pltpu.with_memory_space_constraint(teacher, pltpu.HBM))
     return loss.reshape(n), grad
 
 
 def solution(mesh):
     R, F = mesh.shape["rows"], mesh.shape["feat"]
-    body = functools.partial(fused, R, F) if 2 <= R <= ROWS_LIMIT and F == 4 else ring
+    body = functools.partial(fused, R, F) if 3 <= R <= ROWS_LIMIT and F == 4 else ring
     in_specs = (P(("groups", "rows"), "feat"), P(("groups", "rows"), "feat"))
     out_specs = (P(("groups", "rows")), P(("groups", "rows"), "feat"))
     return jax.shard_map(

time: 42.1 us -> 40.4 us (0.960)
  local copies, waits for them, and re-layouts: 3.37 us -> 1.4 us
  Pallas kernels: 37.8 us -> 38.3 us
    unnamed x6 -> x2, local copies, waits for them, and re-layouts: 3.37 us -> 1.4 us
where the time goes in v3:
time: 40.4 us; the launch traced here: 40.3 us
  Pallas kernels  38.3 us (95%)
  local copies, waits for them, and re-layouts  1.4 us (3%)
  between operations  0.64 us (2%)
    pallas_call x1, Pallas kernels, fused(): pl.pallas_call(functools.partial(kernel, R, F, C), out_shape=(jax.ShapeDt...  38.3 us
    unnamed x2, local copies, waits for them, and re-layouts  1.4 us

profile of v3, /device:TPU:0, one launch (start us, length us, event | category | flops | bytes accessed | tf_op | source)
XLA Modules:
  0.0 40.3 jit_solution(17477118888341363828)
XLA Ops:
  0.6 38.3 %shard_map.41 = (f32[1,160]{1,0:T(1,128)S(1)}, f32[160,1024]{1,0:T(8,128)S(1)}) custom-call(f32[160,1024]{1,0:T(8,128)} %x_hbm.1, bf16[160,256]{1,0:T(8,128)(2,1)} %t_hbm.1), custom_call_target="tpu_custom_call" | custom-call | tf_op jit(solution)/shard_map/pallas_call | solution.py:381
  38.9 0.6 %copy.6 = f32[160]{0:T(256)} copy(f32[160]{0:T(256)S(1)} %bitcast.1) | data formatting | bytes 1280
  39.5 0.8 %copy.7 = f32[160,1024]{1,0:T(8,128)} copy(f32[160,1024]{1,0:T(8,128)S(1)} %get-tuple-element.9) | data formatting | bytes 1310720

commit v4 on v3

--- a/solution.py
+++ b/solution.py
@@ -98,8 +98,8 @@
 
     x_in = pltpu.make_async_copy(x_hbm, x_ref, ins.at[0])
     t_in = pltpu.make_async_copy(t_hbm, t_ref, ins.at[1])
+    t_in.start()
     x_in.start()
-    t_in.start()
 
     eye = lax.broadcasted_iota(jnp.int32, (n, n), 0) == lax.broadcasted_iota(
         jnp.int32, (n, n), 1
@@ -111,9 +111,6 @@
     def to_column(row):
         return jnp.sum(jnp.where(eye, row, 0.0), axis=1, keepdims=True)
 
-    x_in.wait()
-    x = x_ref[...]
-    SQ[f] = jnp.broadcast_to(to_row(jnp.sum(x * x, axis=1, keepdims=True)), (8, n))
     t_in.wait()
     T[z] = t_ref[...]
     pl.semaphore_wait(
@@ -185,8 +182,6 @@
     def u_copy(d, k, c, src):
         return along(U, d, src, (c,), (k, c), us, ur)
 
-    squares_of = lambda g: SQ.at[g]
-    spread(squares_of, (), qs, qr)
     for d in range(2):
         here, src = sends(d, 0)
 
@@ -194,6 +189,11 @@
         def _(d=d, src=src):
             t_copy(d, 0, src).start()
 
+    x_in.wait()
+    x = x_ref[...]
+    SQ[f] = jnp.broadcast_to(to_row(jnp.sum(x * x, axis=1, keepdims=True)), (8, n))
+    squares_of = lambda g: SQ.at[g]
+    spread(squares_of, (), qs, qr)
     collect(squares_of, (), qs, qr)
     squares = SQ[0]
     for g in range(1, F):

time: 40.4 us -> 40.6 us (level)
  no operation moved by 1% of the time
where the time goes in v4:
time: 40.6 us; the launch traced here: 40.4 us
  Pallas kernels  38.4 us (95%)
  local copies, waits for them, and re-layouts  1.4 us (3%)
  between operations  0.64 us (2%)
    pallas_call x1, Pallas kernels, fused(): pl.pallas_call(functools.partial(kernel, R, F, C), out_shape=(jax.ShapeDt...  38.4 us
    unnamed x2, local copies, waits for them, and re-layouts  1.4 us

profile of v4, /device:TPU:0, one launch (start us, length us, event | category | flops | bytes accessed | tf_op | source)
XLA Modules:
  0.0 40.4 jit_solution(16168394046187164462)
XLA Ops:
  0.6 38.4 %shard_map.41 = (f32[1,160]{1,0:T(1,128)S(1)}, f32[160,1024]{1,0:T(8,128)S(1)}) custom-call(f32[160,1024]{1,0:T(8,128)} %x_hbm.1, bf16[160,256]{1,0:T(8,128)(2,1)} %t_hbm.1), custom_call_target="tpu_custom_call" | custom-call | tf_op jit(solution)/shard_map/pallas_call | solution.py:381
  39.0 0.6 %copy.6 = f32[160]{0:T(256)} copy(f32[160]{0:T(256)S(1)} %bitcast.1) | data formatting | bytes 1280
  39.6 0.8 %copy.7 = f32[160,1024]{1,0:T(8,128)} copy(f32[160,1024]{1,0:T(8,128)S(1)} %get-tuple-element.9) | data formatting | bytes 1310720
